TPU v7x, 128 devices: a whole 4x4x4 slice. The times are simulated.
128 devices in a mesh: dp: 8 (over z, x_hi), ctx: 16 (over x_lo, y, core).
Axes of the slice: x: 4 (x_hi: 2, x_lo: 2; x = x_hi * 2 + x_lo), y: 4, z: 4, core: 2. Of those that a mesh axis runs over, the one named last changes fastest.
Arguments:
- events: bfloat16 [65536, 1024], P(('dp', 'ctx')), parts along dimension 0, may hold values from -48 to 48
- destination: int32 [65536], P(('dp', 'ctx')), parts along dimension 0, may hold values from 0 to 8191, as said below
- segment: int32 [65536], P(('dp', 'ctx')), parts along dimension 0, may hold values from 0 to 3, never falling along the last dimension, each value on 1 to 6144 neighbouring positions
- w_query: bfloat16 [1024, 1024], replicated, may hold values from -0.375 to 0.375
- key_weight: bfloat16 [1024, 256], replicated, may hold values from -0.1875 to 0.1875
- value_weight: bfloat16 [1024, 256], replicated, may hold values from -0.75 to 0.75
Outputs:
- attended: bfloat16 [65536, 1024], P(('dp', 'ctx')), parts along dimension 0
There are 8 independent parts, one for each index of `dp`. A program takes and returns all parts, laid end to end along the dimension named above; an argument that names none is the same for every part. Nothing has to cross between parts.
Inputs may be any that keep to these rules, and one draw needn't show every extreme that they name: destination is a permutation that moves stored events in aligned blocks of 64 rows, keeping their order inside a block; the 8 blocks of one device land on 8 different devices' ranges of 512 packed positions, so at most 64 rows of one device reach one device's range.
All inputs are finite; a program needn't handle non-finite values.
Results may differ from a plain program's by a relative error of at most 0.0045.
The roundings to bfloat16 on the way count: a program that leaves them out, or rounds other values in their place, can miss the bound.
Values may be sent and summed in bfloat16 or wider, within the bound.
No kernel may reach another device: no remote copies, remote signals or barrier semaphores. Data moves between devices by JAX's collectives and lax.ppermute only.
A program may use at most 64 MiB of HBM per device.

v0:
```python
import math
import jax
import jax.numpy as jnp
from jax import lax
from jax.sharding import PartitionSpec as P

QUERY_HEADS = 8
KEY_VALUE_HEADS = 2
HEAD_SIZE = 128
BLOCKS = 8
NEGATIVE_FILL = -1e30


def on_device(events, destination, segment, w_query, key_weight, value_weight):
    token_count = events.shape[0]
    width = events.shape[1]
    ndevices = lax.axis_size("ctx")
    myself = lax.axis_index("ctx")
    group_size = QUERY_HEADS // KEY_VALUE_HEADS
    score_scale = 1.0 / math.sqrt(HEAD_SIZE)
    lanes = jnp.arange(ndevices, dtype=jnp.int32)
    local_rows = jnp.arange(token_count, dtype=jnp.int32)
    target = destination // token_count
    place = destination % token_count
    bucket = token_count // BLOCKS
    own_position = myself * token_count + local_rows
    onehot = (target[:, None] == lanes[None, :]).astype(jnp.int32)
    before = jnp.cumsum(onehot, axis=0) - onehot
    slot = jnp.sum(before * onehot, axis=1)
    index = target * bucket + slot
    send_rows = (
        jnp.zeros((ndevices * bucket, width), events.dtype)
        .at[index]
        .set(events)
        .reshape(ndevices, bucket, width)
    )
    send_place = (
        jnp.full((ndevices * bucket,), token_count, jnp.int32)
        .at[index]
        .set(place)
        .reshape(ndevices, bucket)
    )
    got_rows, got_place = (
        lax.all_to_all(send_rows, "ctx", split_axis=0, concat_axis=0, tiled=True),
        lax.all_to_all(send_place, "ctx", split_axis=0, concat_axis=0, tiled=True),
    )
    packed = (
        jnp.zeros((token_count, width), events.dtype)
        .at[got_place.reshape(-1)]
        .set(got_rows.reshape(-1, width), mode="drop")
    )
    query_rows = jnp.dot(packed, w_query, preferred_element_type=jnp.float32).astype(jnp.bfloat16)
    key_rows = jnp.dot(packed, key_weight, preferred_element_type=jnp.float32).astype(jnp.bfloat16)
    value_rows = jnp.dot(packed, value_weight, preferred_element_type=jnp.float32).astype(
        jnp.bfloat16
    )
    query_head_rows = query_rows.reshape(token_count, KEY_VALUE_HEADS, group_size, HEAD_SIZE)
    query_seg = segment.astype(jnp.float32)
    seg_sent = segment.astype(jnp.bfloat16)
    start_state = (
        jnp.full((KEY_VALUE_HEADS, group_size, token_count), NEGATIVE_FILL, jnp.float32),
        jnp.zeros((KEY_VALUE_HEADS, group_size, token_count), jnp.float32),
        jnp.zeros((KEY_VALUE_HEADS, group_size, token_count, HEAD_SIZE), jnp.float32),
    )
    carry = start_state
    key_portion = lax.all_gather(key_rows, "ctx", axis=0, tiled=True)
    value_portion = lax.all_gather(value_rows, "ctx", axis=0, tiled=True)
    seg_piece = lax.all_gather(seg_sent, "ctx", axis=0, tiled=True)
    token_rows = key_portion.shape[0]
    block_step = 512
    event_count = token_rows // block_step
    key_block_list = key_portion.reshape(event_count, block_step, KEY_VALUE_HEADS, HEAD_SIZE)
    value_block_list = value_portion.reshape(event_count, block_step, KEY_VALUE_HEADS, HEAD_SIZE)
    seg_blocks = seg_piece.astype(jnp.float32).reshape(event_count, block_step)
    offsets = jnp.arange(event_count, dtype=jnp.int32) * block_step

    def one_block(state, inputs):
        key_tile_rows, value_block, seg_block, offset = inputs
        key_pos = offset + jnp.arange(block_step, dtype=jnp.int32)
        allowed = (seg_block[None, :] == query_seg[:, None]) & (
            key_pos[None, :] <= own_position[:, None]
        )
        best, total_tokens, accum = state
        logit_scores = (
            jnp.einsum(
                "qxli,oxi->xlqo", query_head_rows, key_tile_rows, preferred_element_type=jnp.float32
            )
            * score_scale
        )
        logit_scores = jnp.where(allowed, logit_scores, NEGATIVE_FILL)
        fresh = jnp.maximum(best, jnp.max(logit_scores, axis=-1))
        softmax_weights = jnp.where(allowed, jnp.exp(logit_scores - fresh[..., None]), 0.0)
        shrink = jnp.exp(best - fresh)
        total_tokens = total_tokens * shrink + jnp.sum(softmax_weights, axis=-1)
        accum = accum * shrink[..., None] + jnp.einsum(
            "qlwc,cqh->qlwh",
            softmax_weights.astype(jnp.bfloat16),
            value_block,
            preferred_element_type=jnp.float32,
        )
        state = (fresh, total_tokens, accum)
        return (state, None)

    carry, _ = lax.scan(one_block, carry, (key_block_list, value_block_list, seg_blocks, offsets))
    best, total_tokens, accum = carry
    result = (
        (accum / total_tokens[..., None])
        .transpose(2, 0, 1, 3)
        .reshape(token_count, QUERY_HEADS * HEAD_SIZE)
        .astype(jnp.bfloat16)
    )
    return result


def solution(mesh):
    return jax.shard_map(
        on_device,
        mesh=mesh,
        in_specs=(P(("dp", "ctx"), None), P(("dp", "ctx")), P(("dp", "ctx")), P(), P(), P()),
        out_specs=P(("dp", "ctx"), None),
        check_vma=False,
    )
```

profile of v0, /device:TPU:1, one launch (start us, length us, event | category | flops | bytes accessed | tf_op | source)
XLA Modules:
  0.0 347.3 jit_solution(6097771895671642066)
XLA Ops:
  8.9 2.4 scatter_custom_fusion
  12.0 6.9 %all-to-all-start = ((s32[16,1,64]{2,1,0:T(1,128)}), s32[16,1,64]{2,1,0:T(1,128)S(1)}, u32[]{:S(2)}, u32[]{:S(2)}) async-start(s32[16,1,64]{2,1,0:T(1,128)} %all_to_all.9), calls=%async_computation | async-start | bytes 16384 | tf_op jit(solution)/shard_map/all_to_all | solution.py:45
  18.9 4.8 %scatter_custom_fusion.1 = bf16[1024,1024]{1,0:T(8,128)(2,1)} fusion(s32[512]{0:T(512)S(1)} %compare_select_fusion.1, bf16[512,1024]{1,0:T(8,128)(2,1)} %param.8, bf16[]{:T(256)} %constant.62.clone.1), kind=kCustom, calls=%fused_computation.33 | custom fusion | bytes 2097664 | tf_op jit(solution)/shard_map/scatter | solution.py:34
  24.4 5.2 %all-to-all-start.1 = ((bf16[16,64,1024]{2,1,0:T(8,128)(2,1)}), bf16[16,64,1024]{2,1,0:T(8,128)(2,1)}, u32[]{:S(2)}, u32[]{:S(2)}) async-start(bf16[16,64,1024]{2,1,0:T(8,128)(2,1)} %bitcast.83), calls=%async_computation.1 | async-start | bytes 4194304 | tf_op jit(solution)/shard_map/all_to_all | solution.py:44
  30.9 26.4 %all-to-all-done.1 = bf16[16,64,1024]{2,1,0:T(8,128)(2,1)} async-done(((bf16[16,64,1024]{2,1,0:T(8,128)(2,1)}), bf16[16,64,1024]{2,1,0:T(8,128)(2,1)}, u32[]{:S(2)}, u32[]{:S(2)}) %all-to-all-start.1) | async-done | bytes 2097184 | tf_op jit(solution)/shard_map/all_to_all | solution.py:44
  57.3 6.2 %scatter_custom_fusion.2 = bf16[512,1024]{1,0:T(8,128)(2,1)S(1)} fusion(s32[1024]{0:T(1024)S(1)} %bitcast.87, bf16[1024,1024]{1,0:T(8,128)(2,1)} %bitcast.4, bf16[]{:T(256)} %constant.62.clone.1), kind=kCustom, calls=%fused_computation.36 | custom fusion | bytes 1049088 | tf_op jit(solution)/shard_map/scatter | solution.py:50
  63.4 2.2 convolution_convert_fusion.1
  65.7 2.2 convolution_convert_fusion.2
  68.0 21.0 %all-gather = bf16[16,1,512]{2,1,0:T(2,128)(2,1)S(1)} all-gather(bf16[1,1,512]{2,1,0:T(2,128)(2,1)S(1)} %reshape.121), channel_id=1, replica_groups=mesh['dp'=8,'ctx'=16] {'ctx'}, dimensions={0}, use_global_device_ids=true | all-gather | bytes 17408 | tf_op jit(solution)/shard_map/all_gather | solution.py:68
  89.0 2.2 convolution_convert_fusion
  91.2 2.6 reshape.91
  95.2 11.1 %all-gather.6.cloned.1.call-done = bf16[8192,256]{1,0:T(8,128)(2,1)} async-done(((bf16[512,256]{1,0:T(8,128)(2,1)}), bf16[8192,256]{1,0:T(8,128)(2,1)}) %all-gather.6.cloned.1.call-update) | async-done | bytes 4194320 | tf_op jit(solution)/shard_map/all_gather | solution.py:67
  106.3 6.9 %reshape.92 = bf16[16,512,2,128]{3,2,1,0:T(2,128)(2,1)} reshape(bf16[8192,256]{1,0:T(8,128)(2,1)} %all-gather.6.cloned.1.call-done) | data formatting | bytes 8388608 | tf_op jit(solution)/shard_map/reshape | solution.py:73
  113.2 31.8 %all-gather.4.cloned.1.call-done = bf16[8192,256]{1,0:T(8,128)(2,1)} async-done(((bf16[512,256]{1,0:T(8,128)(2,1)}), bf16[8192,256]{1,0:T(8,128)(2,1)}) %all-gather.4.cloned.1.call-update) | async-done | bytes 4194320 | tf_op jit(solution)/shard_map/all_gather | solution.py:66
  145.0 6.9 %reshape.90 = bf16[16,512,2,128]{3,2,1,0:T(2,128)(2,1)} reshape(bf16[8192,256]{1,0:T(8,128)(2,1)} %all-gather.4.cloned.1.call-done) | data formatting | bytes 8388608 | tf_op jit(solution)/shard_map/reshape | solution.py:72
  151.9 184.2 %while.15 = (s32[]{:T(128)}, f32[2,4,512]{2,1,0:T(4,128)S(1)}, f32[2,4,512]{2,1,0:T(4,128)S(1)}, f32[2,4,512,128]{3,2,1,0:T(8,128)}, f32[16,512]{1,0:T(8,128)S(1...) while((s32[]{:T(128)}, f32[2,4,512]{2,1,0:T(4,128)S(1)}, ...), condition=%wide.region_9.10_spmd.clone, body=%wide.region_6.9_spmd.clone.sunk | while | flops 1103385600 | bytes 50086116 | solution.py:104
  156.5 2.0 fusion.45
  158.5 3.5 %fusion.47 = f32[2,4,512,128]{3,2,1,0:T(8,128)S(1)} fusion(f32[2,4,512,128]{3,2,1,0:T(8,128)S(1)} %copy-done.1, f32[2,512,512,4]{2,1,3,0:T(8,128)S(1)} %get-tuple-element.250, f32[2,4,512]{2,1,0:T(4,128)S(1)} %select_maximum_fusion.2, pred[512,512]{0,1:T(8,128)(4,1)S(1)} %compare_and_fusion.2, f32[2,4,512]{2,1,0:T(4,128)S(1)} %get-tuple-element.252, ...), kind=kOutput, calls=%fused_computation.12.clone.1 | convolution fusion | flops 548929536 | bytes 13139969 | tf_op jit(solution)/shard_map/while/body/eval_jaxpr/qlwc,cqh->qlwh/dot_general | solution.py:95
  168.0 2.0 fusion.45
  170.1 3.5 %fusion.47 = f32[2,4,512,128]{3,2,1,0:T(8,128)S(1)} fusion(f32[2,4,512,128]{3,2,1,0:T(8,128)S(1)} %copy-done.1, f32[2,512,512,4]{2,1,3,0:T(8,128)S(1)} %get-tuple-element.250, f32[2,4,512]{2,1,0:T(4,128)S(1)} %select_maximum_fusion.2, pred[512,512]{0,1:T(8,128)(4,1)S(1)} %compare_and_fusion.2, f32[2,4,512]{2,1,0:T(4,128)S(1)} %get-tuple-element.252, ...), kind=kOutput, calls=%fused_computation.12.clone.1 | convolution fusion | flops 548929536 | bytes 13139969 | tf_op jit(solution)/shard_map/while/body/eval_jaxpr/qlwc,cqh->qlwh/dot_general | solution.py:95
  179.5 2.0 fusion.45
  181.6 3.5 %fusion.47 = f32[2,4,512,128]{3,2,1,0:T(8,128)S(1)} fusion(f32[2,4,512,128]{3,2,1,0:T(8,128)S(1)} %copy-done.1, f32[2,512,512,4]{2,1,3,0:T(8,128)S(1)} %get-tuple-element.250, f32[2,4,512]{2,1,0:T(4,128)S(1)} %select_maximum_fusion.2, pred[512,512]{0,1:T(8,128)(4,1)S(1)} %compare_and_fusion.2, f32[2,4,512]{2,1,0:T(4,128)S(1)} %get-tuple-element.252, ...), kind=kOutput, calls=%fused_computation.12.clone.1 | convolution fusion | flops 548929536 | bytes 13139969 | tf_op jit(solution)/shard_map/while/body/eval_jaxpr/qlwc,cqh->qlwh/dot_general | solution.py:95
  191.0 2.0 fusion.45
  193.1 3.5 %fusion.47 = f32[2,4,512,128]{3,2,1,0:T(8,128)S(1)} fusion(f32[2,4,512,128]{3,2,1,0:T(8,128)S(1)} %copy-done.1, f32[2,512,512,4]{2,1,3,0:T(8,128)S(1)} %get-tuple-element.250, f32[2,4,512]{2,1,0:T(4,128)S(1)} %select_maximum_fusion.2, pred[512,512]{0,1:T(8,128)(4,1)S(1)} %compare_and_fusion.2, f32[2,4,512]{2,1,0:T(4,128)S(1)} %get-tuple-element.252, ...), kind=kOutput, calls=%fused_computation.12.clone.1 | convolution fusion | flops 548929536 | bytes 13139969 | tf_op jit(solution)/shard_map/while/body/eval_jaxpr/qlwc,cqh->qlwh/dot_general | solution.py:95
  202.5 2.0 fusion.45
  204.6 3.5 %fusion.47 = f32[2,4,512,128]{3,2,1,0:T(8,128)S(1)} fusion(f32[2,4,512,128]{3,2,1,0:T(8,128)S(1)} %copy-done.1, f32[2,512,512,4]{2,1,3,0:T(8,128)S(1)} %get-tuple-element.250, f32[2,4,512]{2,1,0:T(4,128)S(1)} %select_maximum_fusion.2, pred[512,512]{0,1:T(8,128)(4,1)S(1)} %compare_and_fusion.2, f32[2,4,512]{2,1,0:T(4,128)S(1)} %get-tuple-element.252, ...), kind=kOutput, calls=%fused_computation.12.clone.1 | convolution fusion | flops 548929536 | bytes 13139969 | tf_op jit(solution)/shard_map/while/body/eval_jaxpr/qlwc,cqh->qlwh/dot_general | solution.py:95
  214.0 2.0 fusion.45
  216.1 3.5 %fusion.47 = f32[2,4,512,128]{3,2,1,0:T(8,128)S(1)} fusion(f32[2,4,512,128]{3,2,1,0:T(8,128)S(1)} %copy-done.1, f32[2,512,512,4]{2,1,3,0:T(8,128)S(1)} %get-tuple-element.250, f32[2,4,512]{2,1,0:T(4,128)S(1)} %select_maximum_fusion.2, pred[512,512]{0,1:T(8,128)(4,1)S(1)} %compare_and_fusion.2, f32[2,4,512]{2,1,0:T(4,128)S(1)} %get-tuple-element.252, ...), kind=kOutput, calls=%fused_computation.12.clone.1 | convolution fusion | flops 548929536 | bytes 13139969 | tf_op jit(solution)/shard_map/while/body/eval_jaxpr/qlwc,cqh->qlwh/dot_general | solution.py:95
  225.6 2.0 fusion.45
  227.6 3.5 %fusion.47 = f32[2,4,512,128]{3,2,1,0:T(8,128)S(1)} fusion(f32[2,4,512,128]{3,2,1,0:T(8,128)S(1)} %copy-done.1, f32[2,512,512,4]{2,1,3,0:T(8,128)S(1)} %get-tuple-element.250, f32[2,4,512]{2,1,0:T(4,128)S(1)} %select_maximum_fusion.2, pred[512,512]{0,1:T(8,128)(4,1)S(1)} %compare_and_fusion.2, f32[2,4,512]{2,1,0:T(4,128)S(1)} %get-tuple-element.252, ...), kind=kOutput, calls=%fused_computation.12.clone.1 | convolution fusion | flops 548929536 | bytes 13139969 | tf_op jit(solution)/shard_map/while/body/eval_jaxpr/qlwc,cqh->qlwh/dot_general | solution.py:95
  237.1 2.0 fusion.45
  239.2 3.5 %fusion.47 = f32[2,4,512,128]{3,2,1,0:T(8,128)S(1)} fusion(f32[2,4,512,128]{3,2,1,0:T(8,128)S(1)} %copy-done.1, f32[2,512,512,4]{2,1,3,0:T(8,128)S(1)} %get-tuple-element.250, f32[2,4,512]{2,1,0:T(4,128)S(1)} %select_maximum_fusion.2, pred[512,512]{0,1:T(8,128)(4,1)S(1)} %compare_and_fusion.2, f32[2,4,512]{2,1,0:T(4,128)S(1)} %get-tuple-element.252, ...), kind=kOutput, calls=%fused_computation.12.clone.1 | convolution fusion | flops 548929536 | bytes 13139969 | tf_op jit(solution)/shard_map/while/body/eval_jaxpr/qlwc,cqh->qlwh/dot_general | solution.py:95
  248.6 2.0 fusion.45
  250.7 3.5 %fusion.47 = f32[2,4,512,128]{3,2,1,0:T(8,128)S(1)} fusion(f32[2,4,512,128]{3,2,1,0:T(8,128)S(1)} %copy-done.1, f32[2,512,512,4]{2,1,3,0:T(8,128)S(1)} %get-tuple-element.250, f32[2,4,512]{2,1,0:T(4,128)S(1)} %select_maximum_fusion.2, pred[512,512]{0,1:T(8,128)(4,1)S(1)} %compare_and_fusion.2, f32[2,4,512]{2,1,0:T(4,128)S(1)} %get-tuple-element.252, ...), kind=kOutput, calls=%fused_computation.12.clone.1 | convolution fusion | flops 548929536 | bytes 13139969 | tf_op jit(solution)/shard_map/while/body/eval_jaxpr/qlwc,cqh->qlwh/dot_general | solution.py:95
  260.1 2.0 fusion.45
  262.2 3.5 %fusion.47 = f32[2,4,512,128]{3,2,1,0:T(8,128)S(1)} fusion(f32[2,4,512,128]{3,2,1,0:T(8,128)S(1)} %copy-done.1, f32[2,512,512,4]{2,1,3,0:T(8,128)S(1)} %get-tuple-element.250, f32[2,4,512]{2,1,0:T(4,128)S(1)} %select_maximum_fusion.2, pred[512,512]{0,1:T(8,128)(4,1)S(1)} %compare_and_fusion.2, f32[2,4,512]{2,1,0:T(4,128)S(1)} %get-tuple-element.252, ...), kind=kOutput, calls=%fused_computation.12.clone.1 | convolution fusion | flops 548929536 | bytes 13139969 | tf_op jit(solution)/shard_map/while/body/eval_jaxpr/qlwc,cqh->qlwh/dot_general | solution.py:95
  271.6 2.0 fusion.45
  273.7 3.5 %fusion.47 = f32[2,4,512,128]{3,2,1,0:T(8,128)S(1)} fusion(f32[2,4,512,128]{3,2,1,0:T(8,128)S(1)} %copy-done.1, f32[2,512,512,4]{2,1,3,0:T(8,128)S(1)} %get-tuple-element.250, f32[2,4,512]{2,1,0:T(4,128)S(1)} %select_maximum_fusion.2, pred[512,512]{0,1:T(8,128)(4,1)S(1)} %compare_and_fusion.2, f32[2,4,512]{2,1,0:T(4,128)S(1)} %get-tuple-element.252, ...), kind=kOutput, calls=%fused_computation.12.clone.1 | convolution fusion | flops 548929536 | bytes 13139969 | tf_op jit(solution)/shard_map/while/body/eval_jaxpr/qlwc,cqh->qlwh/dot_general | solution.py:95
  283.1 2.0 fusion.45
  285.2 3.5 %fusion.47 = f32[2,4,512,128]{3,2,1,0:T(8,128)S(1)} fusion(f32[2,4,512,128]{3,2,1,0:T(8,128)S(1)} %copy-done.1, f32[2,512,512,4]{2,1,3,0:T(8,128)S(1)} %get-tuple-element.250, f32[2,4,512]{2,1,0:T(4,128)S(1)} %select_maximum_fusion.2, pred[512,512]{0,1:T(8,128)(4,1)S(1)} %compare_and_fusion.2, f32[2,4,512]{2,1,0:T(4,128)S(1)} %get-tuple-element.252, ...), kind=kOutput, calls=%fused_computation.12.clone.1 | convolution fusion | flops 548929536 | bytes 13139969 | tf_op jit(solution)/shard_map/while/body/eval_jaxpr/qlwc,cqh->qlwh/dot_general | solution.py:95
  294.7 2.0 fusion.45
  296.7 3.5 %fusion.47 = f32[2,4,512,128]{3,2,1,0:T(8,128)S(1)} fusion(f32[2,4,512,128]{3,2,1,0:T(8,128)S(1)} %copy-done.1, f32[2,512,512,4]{2,1,3,0:T(8,128)S(1)} %get-tuple-element.250, f32[2,4,512]{2,1,0:T(4,128)S(1)} %select_maximum_fusion.2, pred[512,512]{0,1:T(8,128)(4,1)S(1)} %compare_and_fusion.2, f32[2,4,512]{2,1,0:T(4,128)S(1)} %get-tuple-element.252, ...), kind=kOutput, calls=%fused_computation.12.clone.1 | convolution fusion | flops 548929536 | bytes 13139969 | tf_op jit(solution)/shard_map/while/body/eval_jaxpr/qlwc,cqh->qlwh/dot_general | solution.py:95
  306.2 2.0 fusion.45
  308.3 3.5 %fusion.47 = f32[2,4,512,128]{3,2,1,0:T(8,128)S(1)} fusion(f32[2,4,512,128]{3,2,1,0:T(8,128)S(1)} %copy-done.1, f32[2,512,512,4]{2,1,3,0:T(8,128)S(1)} %get-tuple-element.250, f32[2,4,512]{2,1,0:T(4,128)S(1)} %select_maximum_fusion.2, pred[512,512]{0,1:T(8,128)(4,1)S(1)} %compare_and_fusion.2, f32[2,4,512]{2,1,0:T(4,128)S(1)} %get-tuple-element.252, ...), kind=kOutput, calls=%fused_computation.12.clone.1 | convolution fusion | flops 548929536 | bytes 13139969 | tf_op jit(solution)/shard_map/while/body/eval_jaxpr/qlwc,cqh->qlwh/dot_general | solution.py:95
  317.7 2.0 fusion.45
  319.8 3.5 %fusion.47 = f32[2,4,512,128]{3,2,1,0:T(8,128)S(1)} fusion(f32[2,4,512,128]{3,2,1,0:T(8,128)S(1)} %copy-done.1, f32[2,512,512,4]{2,1,3,0:T(8,128)S(1)} %get-tuple-element.250, f32[2,4,512]{2,1,0:T(4,128)S(1)} %select_maximum_fusion.2, pred[512,512]{0,1:T(8,128)(4,1)S(1)} %compare_and_fusion.2, f32[2,4,512]{2,1,0:T(4,128)S(1)} %get-tuple-element.252, ...), kind=kOutput, calls=%fused_computation.12.clone.1 | convolution fusion | flops 548929536 | bytes 13139969 | tf_op jit(solution)/shard_map/while/body/eval_jaxpr/qlwc,cqh->qlwh/dot_general | solution.py:95
  329.2 2.0 fusion.45
  331.3 3.5 %fusion.47 = f32[2,4,512,128]{3,2,1,0:T(8,128)S(1)} fusion(f32[2,4,512,128]{3,2,1,0:T(8,128)S(1)} %copy-done.1, f32[2,512,512,4]{2,1,3,0:T(8,128)S(1)} %get-tuple-element.250, f32[2,4,512]{2,1,0:T(4,128)S(1)} %select_maximum_fusion.2, pred[512,512]{0,1:T(8,128)(4,1)S(1)} %compare_and_fusion.2, f32[2,4,512]{2,1,0:T(4,128)S(1)} %get-tuple-element.252, ...), kind=kOutput, calls=%fused_computation.12.clone.1 | convolution fusion | flops 548929536 | bytes 13139969 | tf_op jit(solution)/shard_map/while/body/eval_jaxpr/qlwc,cqh->qlwh/dot_general | solution.py:95
  (241 shorter events, 104.9 us)
Async XLA Ops:
  6.5 82.5 %copy-start = (bf16[1024,1024]{1,0:T(8,128)(2,1)S(1)}, bf16[1024,1024]{1,0:T(8,128)(2,1)}, u32[]{:S(2)}) copy-start(bf16[1024,1024]{1,0:T(8,128)(2,1)} %param.11) | copy-start | bytes 6291460
  12.0 12.3 %all-to-all-start = ((s32[16,1,64]{2,1,0:T(1,128)}), s32[16,1,64]{2,1,0:T(1,128)S(1)}, u32[]{:S(2)}, u32[]{:S(2)}) async-start(s32[16,1,64]{2,1,0:T(1,128)} %all_to_all.9), calls=%async_computation | async-start | bytes 16384 | tf_op jit(solution)/shard_map/all_to_all | solution.py:45
  24.4 43.6 %copy-start.3 = (s32[512]{0:T(512)S(1)}, s32[512]{0:T(512)}, u32[]{:S(2)}) copy-start(s32[512]{0:T(512)} %param.10) | copy-start | bytes 6148
  24.4 32.9 %all-to-all-start.1 = ((bf16[16,64,1024]{2,1,0:T(8,128)(2,1)}), bf16[16,64,1024]{2,1,0:T(8,128)(2,1)}, u32[]{:S(2)}, u32[]{:S(2)}) async-start(bf16[16,64,1024]{2,1,0:T(8,128)(2,1)} %bitcast.83), calls=%async_computation.1 | async-start | bytes 4194304 | tf_op jit(solution)/shard_map/all_to_all | solution.py:44
  29.6 76.7 %all-gather.6.cloned.1.call-start = ((), (), s32[]{:S(2)}) async-start(), calls=%async_computation.3 | async-start | bytes 4456448 | tf_op jit(solution)/shard_map/all_gather | solution.py:67
  65.7 79.3 %all-gather.4.cloned.1.call-start = ((), (), s32[]{:S(2)}) async-start(), calls=%async_computation.2 | async-start | bytes 4456448 | tf_op jit(solution)/shard_map/all_gather | solution.py:66
  156.4 2.1 copy-start.1
  162.1 1.4 copy-start.2
  168.0 2.1 copy-start.1
  173.6 1.4 copy-start.2
  179.5 2.1 copy-start.1
  185.1 1.4 copy-start.2
  191.0 2.1 copy-start.1
  196.6 1.4 copy-start.2
  202.5 2.1 copy-start.1
  208.1 1.4 copy-start.2
  214.0 2.1 copy-start.1
  219.6 1.4 copy-start.2
  225.5 2.1 copy-start.1
  231.2 1.4 copy-start.2
  237.1 2.1 copy-start.1
  242.7 1.4 copy-start.2
  248.6 2.1 copy-start.1
  254.2 1.4 copy-start.2
  260.1 2.1 copy-start.1
  265.7 1.4 copy-start.2
  271.6 2.1 copy-start.1
  277.2 1.4 copy-start.2
  283.1 2.1 copy-start.1
  288.7 1.4 copy-start.2
  294.6 2.1 copy-start.1
  300.3 1.4 copy-start.2
  306.1 2.1 copy-start.1
  311.8 1.4 copy-start.2
  317.7 2.1 copy-start.1
  323.3 1.4 copy-start.2
  329.2 2.1 copy-start.1
  334.8 1.4 copy-start.2
Sparse Core Ops, SparseCore 0:
  65.8 40.4 all-gather.5
  108.0 36.9 all-gather.3
where the time goes:
time: 349 us; the launch traced here: 347 us
  local copies, waits for them, and re-layouts  88.4 us (25%)
  matrix products  88.2 us (25%)
  waiting for transfers between devices  70 us (20%)
  other arithmetic  52.9 us (15%)
  blocking collectives  21 us (6%)
  between operations  13.5 us (4%)
  starting transfers between devices  12.2 us (3%)
    dot_general x16, matrix products, one_block(): jnp.einsum('qlwc,cqh->qlwh', softmax_weights.astype(jnp.bfloat16), value_...  56.2 us
    reduce_sum x16, other arithmetic, one_block(): total_tokens = total_tokens * shrink + jnp.sum(softmax_weights, axis=-1)  32.7 us
    all_gather x1, waiting for transfers between devices, on_device(): key_portion = lax.all_gather(key_rows, 'ctx', axis=0, tiled=True)  31.8 us
    dynamic_slice x48, local copies, waits for them, and re-layouts, on_device(): lax.scan(one_block, carry, (key_block_list, value_block_list, seg_blocks,...  31.8 us
    all_to_all x1, waiting for transfers between devices, on_device(): lax.all_to_all(send_rows, 'ctx', split_axis=0, concat_axis=0, tiled=True)  26.4 us
    dot_general x16, matrix products, one_block(): jnp.einsum('qxli,oxi->xlqo', query_head_rows, key_tile_rows, preferred_el...  25.3 us
    while x80, local copies, waits for them, and re-layouts  21.6 us
    all_gather x1, blocking collectives, on_device(): seg_piece = lax.all_gather(seg_sent, 'ctx', axis=0, tiled=True)  21 us
  transfers between devices with their start and end apart: 4, of which 4 were waited for; matrix products, arithmetic and copies ran while one was open for 6% of the time, Pallas kernels for 0%

commit v1 on v0

--- a/solution.py
+++ b/solution.py
@@ -1,14 +1,24 @@
+import functools
 import math
 import jax
 import jax.numpy as jnp
 from jax import lax
 from jax.sharding import PartitionSpec as P
+from jax.lax import all_to_all, axis_size
 
 QUERY_HEADS = 8
 KEY_VALUE_HEADS = 2
 HEAD_SIZE = 128
 BLOCKS = 8
 NEGATIVE_FILL = -1e30
+
+
+def do_groups(x_in, dim_i):
+    main = jnp.stack([x_in for _ in range(axis_size("ctx"))], 0)
+    return jnp.concatenate(all_to_all(main, split_axis=0, concat_axis=0, axis_name="ctx"), dim_i)
+
+
+trace_the_meshes = functools.partial(do_groups, dim_i=0)
 
 
 def on_device(events, destination, segment, w_query, key_weight, value_weight):
@@ -63,7 +73,7 @@
         jnp.zeros((KEY_VALUE_HEADS, group_size, token_count, HEAD_SIZE), jnp.float32),
     )
     carry = start_state
-    key_portion = lax.all_gather(key_rows, "ctx", axis=0, tiled=True)
+    key_portion = trace_the_meshes(key_rows)
     value_portion = lax.all_gather(value_rows, "ctx", axis=0, tiled=True)
     seg_piece = lax.all_gather(seg_sent, "ctx", axis=0, tiled=True)
     token_rows = key_portion.shape[0]

time: 349 us -> 385 us (1.10)
  blocking collectives: 21 us -> 85.2 us
  waiting for transfers between devices: 70 us -> 27.1 us
  matrix products: 88.2 us -> 104 us
  local copies, waits for them, and re-layouts: 88.4 us -> 79.7 us
  starting transfers between devices: 12.2 us -> 18.4 us
    all_gather x1, blocking collectives: 21 us -> 85.2 us  [on_device(): seg_piece = lax.all_gather(seg_sent, 'ctx', axis=0, tiled=True)]
    all_gather x1 -> x0, waiting for transfers between devices: 31.8 us -> none  [on_device(): key_portion = lax.all_gather(key_rows, 'ctx', axis=0, tiled=True)]
    dot_general x16, matrix products: 25.3 us -> 41.7 us  [one_block(): jnp.einsum('qxli,oxi->xlqo', query_head_rows, key_tile_rows, preferred_el...]
    all_gather x1, waiting for transfers between devices: 11.1 us -> 0.02 us  [on_device(): value_portion = lax.all_gather(value_rows, 'ctx', axis=0, tiled=True)]
    reshape x1 -> x0, local copies, waits for them, and re-layouts: 6.92 us -> none  [on_device(): key_portion.reshape(event_count, block_step, KEY_VALUE_HEADS, HEAD_SIZE)]
    all_to_all x0 -> x1, starting transfers between devices: none -> 6.39 us  [do_groups(): all_to_all(main, split_axis=0, concat_axis=0, axis_name='ctx')]
    dynamic_slice x48, local copies, waits for them, and re-layouts: 31.8 us -> 27.6 us  [on_device(): lax.scan(one_block, carry, (key_block_list, value_block_list, seg_blocks,...]
  transfers between devices with their start and end apart: 4 -> 4, of which waited for: 4 -> 2; matrix products, arithmetic and copies ran while one was open for 6% -> 6% of each run, Pallas kernels for 0% -> 0%
where the time goes in v1:
time: 385 us; the launch traced here: 382 us
  matrix products  104 us (27%)
  blocking collectives  85.2 us (22%)
  local copies, waits for them, and re-layouts  79.7 us (21%)
  other arithmetic  52.9 us (14%)
  waiting for transfers between devices  27.1 us (7%)
  starting transfers between devices  18.4 us (5%)
  between operations  13.6 us (4%)
    all_gather x1, blocking collectives, on_device(): seg_piece = lax.all_gather(seg_sent, 'ctx', axis=0, tiled=True)  85.2 us
    dot_general x16, matrix products, one_block(): jnp.einsum('qlwc,cqh->qlwh', softmax_weights.astype(jnp.bfloat16), value_...  56.2 us
    dot_general x16, matrix products, one_block(): jnp.einsum('qxli,oxi->xlqo', query_head_rows, key_tile_rows, preferred_el...  41.7 us
    reduce_sum x16, other arithmetic, one_block(): total_tokens = total_tokens * shrink + jnp.sum(softmax_weights, axis=-1)  32.7 us
    dynamic_slice x48, local copies, waits for them, and re-layouts, on_device(): lax.scan(one_block, carry, (key_block_list, value_block_list, seg_blocks,...  27.6 us
    all_to_all x1, waiting for transfers between devices, on_device(): lax.all_to_all(send_rows, 'ctx', split_axis=0, concat_axis=0, tiled=True)  26.4 us
    while x80, local copies, waits for them, and re-layouts  21.4 us
    add x16, other arithmetic, on_device(): own_position = myself * token_count + local_rows  10.3 us
  transfers between devices with their start and end apart: 4, of which 2 were waited for; matrix products, arithmetic and copies ran while one was open for 6% of the time, Pallas kernels for 0%

profile of v1, /device:TPU:1, one launch (start us, length us, event | category | flops | bytes accessed | tf_op | source)
XLA Modules:
  0.0 382.2 jit_solution(14803848642137771946)
XLA Ops:
  8.9 2.4 scatter_custom_fusion
  12.0 6.9 %all-to-all-start = ((s32[16,1,64]{2,1,0:T(1,128)}), s32[16,1,64]{2,1,0:T(1,128)S(1)}, u32[]{:S(2)}, u32[]{:S(2)}) async-start(s32[16,1,64]{2,1,0:T(1,128)} %all_to_all.12), calls=%async_computation | async-start | bytes 16384 | tf_op jit(solution)/shard_map/all_to_all | solution.py:55
  18.9 4.8 %scatter_custom_fusion.1 = bf16[1024,1024]{1,0:T(8,128)(2,1)} fusion(s32[512]{0:T(512)S(1)} %compare_select_fusion.1, bf16[512,1024]{1,0:T(8,128)(2,1)} %param.8, bf16[]{:T(256)} %constant.62.clone.1), kind=kCustom, calls=%fused_computation.34 | custom fusion | bytes 2097664 | tf_op jit(solution)/shard_map/scatter | solution.py:44
  24.4 5.1 %all-to-all-start.1 = ((bf16[16,64,1024]{2,1,0:T(8,128)(2,1)}), bf16[16,64,1024]{2,1,0:T(8,128)(2,1)}, u32[]{:S(2)}, u32[]{:S(2)}) async-start(bf16[16,64,1024]{2,1,0:T(8,128)(2,1)} %bitcast.85), calls=%async_computation.1 | async-start | bytes 4194304 | tf_op jit(solution)/shard_map/all_to_all | solution.py:54
  30.8 26.4 %all-to-all-done.1 = bf16[16,64,1024]{2,1,0:T(8,128)(2,1)} async-done(((bf16[16,64,1024]{2,1,0:T(8,128)(2,1)}), bf16[16,64,1024]{2,1,0:T(8,128)(2,1)}, u32[]{:S(2)}, u32[]{:S(2)}) %all-to-all-start.1) | async-done | bytes 2097184 | tf_op jit(solution)/shard_map/all_to_all | solution.py:54
  57.1 6.2 %scatter_custom_fusion.2 = bf16[512,1024]{1,0:T(8,128)(2,1)S(1)} fusion(s32[1024]{0:T(1024)S(1)} %bitcast.89, bf16[1024,1024]{1,0:T(8,128)(2,1)} %bitcast.4, bf16[]{:T(256)} %constant.62.clone.1), kind=kCustom, calls=%fused_computation.37 | custom fusion | bytes 1049088 | tf_op jit(solution)/shard_map/scatter | solution.py:60
  63.3 2.6 convolution_convert_fusion.1
  67.5 2.4 stack.2
  69.9 6.4 %all-to-all-start.2 = ((bf16[16,512,256]{1,2,0:T(8,128)(2,1)}), bf16[16,512,256]{1,2,0:T(8,128)(2,1)}, u32[]{:S(2)}, u32[]{:S(2)}) async-start(bf16[16,512,256]{1,2,0:T(8,128)(2,1)} %stack.2), calls=%async_computation.2 | async-start | bytes 8388608 | tf_op jit(solution)/shard_map/all_to_all | solution.py:18
  76.4 85.2 %all-gather = bf16[16,1,512]{2,1,0:T(2,128)(2,1)S(1)} all-gather(bf16[1,1,512]{2,1,0:T(2,128)(2,1)S(1)} %reshape.119), channel_id=1, replica_groups=mesh['dp'=8,'ctx'=16] {'ctx'}, dimensions={0}, use_global_device_ids=true | all-gather | bytes 17408 | tf_op jit(solution)/shard_map/all_gather | solution.py:78
  161.6 2.2 convolution_convert_fusion
  163.9 2.6 reshape.89
  167.8 6.9 %reshape.90 = bf16[16,512,2,128]{3,2,1,0:T(2,128)(2,1)} reshape(bf16[8192,256]{1,0:T(8,128)(2,1)} %all-gather.3.cloned.1.call-done) | data formatting | bytes 8388608 | tf_op jit(solution)/shard_map/reshape | solution.py:83
  174.8 196.3 %while.15 = (s32[]{:T(128)}, f32[2,4,512]{2,1,0:T(4,128)S(1)}, f32[2,4,512]{2,1,0:T(4,128)S(1)}, f32[2,4,512,128]{3,2,1,0:T(8,128)}, f32[16,512]{1,0:T(8,128)S(1...) while((s32[]{:T(128)}, f32[2,4,512]{2,1,0:T(4,128)S(1)}, ...), condition=%wide.region_9.10_spmd.clone, body=%wide.region_6.9_spmd.clone.sunk | while | flops 1103385600 | bytes 49561832 | solution.py:114
  177.4 2.6 fusion.47
  182.2 3.5 fusion.50
  189.7 2.6 fusion.47
  194.4 3.5 fusion.50
  202.0 2.6 fusion.47
  204.6 2.0 fusion.48
  206.7 3.5 fusion.50
  214.2 2.6 fusion.47
  216.9 2.0 fusion.48
  219.0 3.5 fusion.50
  226.5 2.6 fusion.47
  231.2 3.5 fusion.50
  238.8 2.6 fusion.47
  243.5 3.5 fusion.50
  251.1 2.6 fusion.47
  255.8 3.5 fusion.50
  263.3 2.6 fusion.47
  268.1 3.5 fusion.50
  275.6 2.6 fusion.47
  280.3 3.5 fusion.50
  287.9 2.6 fusion.47
  292.6 3.5 fusion.50
  300.1 2.6 fusion.47
  304.9 3.5 fusion.50
  312.4 2.6 fusion.47
  317.1 3.5 fusion.50
  324.7 2.6 fusion.47
  329.4 3.5 fusion.50
  336.9 2.6 fusion.47
  341.7 3.5 fusion.50
  349.2 2.6 fusion.47
  353.9 3.5 fusion.50
  361.5 2.6 fusion.47
  366.2 3.5 fusion.50
  (245 shorter events, 105.5 us)
Async XLA Ops:
  6.5 155.1 %copy-start = (bf16[1024,1024]{1,0:T(8,128)(2,1)S(1)}, bf16[1024,1024]{1,0:T(8,128)(2,1)}, u32[]{:S(2)}) copy-start(bf16[1024,1024]{1,0:T(8,128)(2,1)} %param.11) | copy-start | bytes 6291460
  12.0 12.3 %all-to-all-start = ((s32[16,1,64]{2,1,0:T(1,128)}), s32[16,1,64]{2,1,0:T(1,128)S(1)}, u32[]{:S(2)}, u32[]{:S(2)}) async-start(s32[16,1,64]{2,1,0:T(1,128)} %all_to_all.12), calls=%async_computation | async-start | bytes 16384 | tf_op jit(solution)/shard_map/all_to_all | solution.py:55
  24.4 32.8 %all-to-all-start.1 = ((bf16[16,64,1024]{2,1,0:T(8,128)(2,1)}), bf16[16,64,1024]{2,1,0:T(8,128)(2,1)}, u32[]{:S(2)}, u32[]{:S(2)}) async-start(bf16[16,64,1024]{2,1,0:T(8,128)(2,1)} %bitcast.85), calls=%async_computation.1 | async-start | bytes 4194304 | tf_op jit(solution)/shard_map/all_to_all | solution.py:54
  29.4 138.4 %all-gather.3.cloned.1.call-start = ((), (), s32[]{:S(2)}) async-start(), calls=%async_computation.3 | async-start | bytes 4456448 | tf_op jit(solution)/shard_map/all_gather | solution.py:77
  63.3 2.6 copy-start.3
  69.9 6.4 %copy-start.5 = (s32[512]{0:T(512)S(1)}, s32[512]{0:T(512)}, u32[]{:S(2)}) copy-start(s32[512]{0:T(512)} %param.10) | copy-start | bytes 6148
  69.9 91.7 %copy-start.4 = (bf16[512,1024]{1,0:T(8,128)(2,1)S(1)}, bf16[512,1024]{1,0:T(8,128)(2,1)}, u32[]{:S(2)}) copy-start(bf16[512,1024]{1,0:T(8,128)(2,1)} %copy-done.3) | copy-start | bytes 3145732
  69.9 104.9 %all-to-all-start.2 = ((bf16[16,512,256]{1,2,0:T(8,128)(2,1)}), bf16[16,512,256]{1,2,0:T(8,128)(2,1)}, u32[]{:S(2)}, u32[]{:S(2)}) async-start(bf16[16,512,256]{1,2,0:T(8,128)(2,1)} %stack.2), calls=%async_computation.2 | async-start | bytes 8388608 | tf_op jit(solution)/shard_map/all_to_all | solution.py:18
  180.1 2.1 copy-start.1
  185.7 1.4 copy-start.2
  192.3 2.1 copy-start.1
  198.0 1.4 copy-start.2
  204.6 2.1 copy-start.1
  210.2 1.4 copy-start.2
  216.9 2.1 copy-start.1
  222.5 1.4 copy-start.2
  229.1 2.1 copy-start.1
  234.8 1.4 copy-start.2
  241.4 2.1 copy-start.1
  247.0 1.4 copy-start.2
  253.7 2.1 copy-start.1
  259.3 1.4 copy-start.2
  266.0 2.1 copy-start.1
  271.6 1.4 copy-start.2
  278.2 2.1 copy-start.1
  283.8 1.4 copy-start.2
  290.5 2.1 copy-start.1
  296.1 1.4 copy-start.2
  302.8 2.1 copy-start.1
  308.4 1.4 copy-start.2
  315.0 2.1 copy-start.1
  320.7 1.4 copy-start.2
  327.3 2.1 copy-start.1
  332.9 1.4 copy-start.2
  339.6 2.1 copy-start.1
  345.2 1.4 copy-start.2
  351.8 2.1 copy-start.1
  357.5 1.4 copy-start.2
  364.1 2.1 copy-start.1
  369.7 1.4 copy-start.2
Sparse Core Ops, SparseCore 0:
  66.0 84.0 all-gather.2
